TPU v7x, 256 devices: a whole 4x4x8 slice. The times are simulated.
256 devices in a mesh: ctx: 16 (over z, core), exp: 16 (over x, y).
Axes of the slice: x: 4, y: 4, z: 8, core: 2. Of those that a mesh axis runs over, the one named last changes fastest.
Arguments:
- inner_input: bfloat16 [8192, 8192], P('ctx', 'exp'), may hold values from -6 to 6
- gate_input: bfloat16 [8192, 8192], P('ctx', 'exp'), may hold values from -6 to 6
- coupling_input: bfloat16 [8192, 256], P('ctx'), may hold values from -6 to 6
- step_input: float32 [8192, 128], P('ctx', 'exp'), may hold values from -7 to 140
- conv_inner: float32 [4, 8192], P(None, 'exp'), may hold values from -3 to 3
- conv_coupling: float32 [4, 256], replicated, may hold values from -3 to 3
- decay_log: float32 [128], P('exp'), may hold values from -5.3 to -2.5
- skip_gain: float32 [128], P('exp'), may hold values from 0.5 to 2
- norm_gain: float32 [8192], P('exp'), may hold values from 0.1 to 1.9
- out_weight: bfloat16 [8192, 4096], P('exp'), may hold values from -0.0625 to 0.0625
- residual: bfloat16 [8192, 4096], P(('ctx', 'exp')), may hold values from -6 to 6
- moe_gain: float32 [4096], replicated, may hold values from 0.1 to 1.9
- router_weight: bfloat16 [4096, 72], replicated, may hold values from -0.1875 to 0.1875
- routes: int32 [8192, 10], P(('ctx', 'exp')), may hold values from 0 to 71, all different within a row
- priority: int32 [256, 32], P(('ctx', 'exp')), may hold values from 0 to 31, each once within a row
- expert_in: bfloat16 [16, 4096, 1536], P('exp', 'ctx'), may hold values from -0.09375 to 0.09375
- expert_out: bfloat16 [16, 4096, 768], P('exp', 'ctx'), may hold values from -0.21875 to 0.21875
Outputs:
- hidden: float32 [8192, 4096], P(('ctx', 'exp'))
- moe_out: float32 [8192, 4096], P(('ctx', 'exp'))
Inputs may be any that keep to these rules, and one draw needn't show every extreme that they name: `routes`: each token names 10 different experts. `priority`: the 32 tokens of each row carry distinct priorities.
All inputs are finite; a program needn't handle non-finite values.
Results may differ from a plain program's by a relative error of at most 0.029.
Values may be sent and summed in bfloat16 or wider, within the bound.
A program may use at most 128 MiB of HBM per device.

v0:
```python
import jax
import jax.numpy as jnp
from jax import lax
from jax.sharding import PartitionSpec as P

HDIM = 64
STATE = 128
KCONV = 4
NEXP = 72
TOPK = 10
FFE = 768
SPAN = 256
INNER = 8192
EPS = 1e-05
HIGH = lax.Precision.HIGHEST


def shifted(array, axis, by):
    devices = lax.axis_size(axis)
    pairs = [(i, i + by) for i in range(devices) if 0 <= i + by < devices]
    return lax.ppermute(array, axis, pairs)


def carried_in(part, axis, combine, identity):
    place = lax.axis_index(axis)
    gathered = jax.tree.map(lambda a: lax.all_gather(a, axis), part)
    state = jax.tree.map(lambda a, e: jnp.zeros_like(a) + jnp.asarray(e, a.dtype), part, identity)

    def one(step, state):
        return combine(
            state, jax.tree.map(lambda a: lax.dynamic_index_in_dim(a, step, 0, False), gathered)
        )

    return lax.fori_loop(0, place, one, state)


def causal_conv(values, before, weight):
    count = values.shape[0]
    padded = jnp.concatenate([before.astype(jnp.float32), values.astype(jnp.float32)], axis=0)
    total = jnp.zeros((count, values.shape[1]), jnp.float32)
    for k in range(KCONV):
        total = total + weight[k][None, :] * padded[k : k + count]
    return jax.nn.silu(total).astype(jnp.bfloat16)


def join_states(earlier, later):
    return (earlier[0] * later[0], later[0][:, None, None] * earlier[1] + later[1])


def body(
    inner_input,
    gate_input,
    coupling_input,
    step_input,
    conv_inner,
    conv_coupling,
    decay_log,
    skip_gain,
    norm_gain,
    out_weight,
    residual,
    moe_gain,
    router_weight,
    routes,
    priority,
    expert_in,
    expert_out,
):
    width = inner_input.shape[1]
    heads = decay_log.shape[0]
    count = inner_input.shape[0]
    blocks = count // SPAN
    edges = jnp.concatenate(
        [inner_input[count - (KCONV - 1) :], coupling_input[count - (KCONV - 1) :]], axis=1
    )
    before = shifted(edges, "ctx", 1)
    inner = causal_conv(inner_input, before[:, :width], conv_inner)
    coupling = causal_conv(coupling_input, before[:, width:], conv_coupling)
    steps = jax.nn.softplus(step_input).reshape(blocks, SPAN, heads)
    inner_parts = inner.reshape(blocks, SPAN, heads, HDIM)
    input_parts = coupling[:, :STATE].reshape(blocks, SPAN, STATE)
    output_parts = coupling[:, STATE:].reshape(blocks, SPAN, STATE)
    rate = steps * (-jnp.exp(decay_log))[None, None, :]
    cums = jnp.cumsum(rate, axis=1)
    scores = jnp.einsum(
        "cin,cjn->cij", output_parts, input_parts, preferred_element_type=jnp.float32
    )
    above = (jnp.arange(SPAN)[:, None] >= jnp.arange(SPAN)[None, :])[None, None]
    flipped = jnp.swapaxes(cums, 1, 2)
    spread = flipped[:, :, :, None] - flipped[:, :, None, :]
    decay = jnp.where(above, jnp.exp(jnp.where(above, spread, 0.0)), 0.0)
    mixing = (scores[:, None] * decay * jnp.swapaxes(steps, 1, 2)[:, :, None, :]).astype(
        jnp.bfloat16
    )
    local = jnp.einsum("chij,cjhp->cihp", mixing, inner_parts, preferred_element_type=jnp.float32)
    inner_wide = inner_parts.astype(jnp.float32)
    tail = jnp.exp(cums[:, -1:, :] - cums) * steps
    states = jnp.einsum(
        "cjh,cjn,cjhp->chnp", tail, input_parts.astype(jnp.float32), inner_wide, precision=HIGH
    )
    drops = jnp.exp(cums[:, -1, :])
    running = jnp.zeros((heads, STATE, HDIM), jnp.float32)
    reach = jnp.ones((heads,), jnp.float32)
    starts = []
    reaches = []
    for k in range(blocks):
        starts.append(running)
        reaches.append(reach)
        running = drops[k][:, None, None] * running + states[k]
        reach = reach * drops[k]
    neutral = (jnp.ones((heads,), jnp.float32), jnp.zeros((heads, STATE, HDIM), jnp.float32))
    incoming = carried_in((reach, running), "ctx", join_states, neutral)[1]
    entry = jnp.stack([reaches[k][:, None, None] * incoming + starts[k] for k in range(blocks)])
    carried = jnp.einsum(
        "cin,cih,chnp->cihp", output_parts.astype(jnp.float32), jnp.exp(cums), entry, precision=HIGH
    )
    mixed = (local + carried + skip_gain[None, None, :, None] * inner_wide).reshape(count, width)
    gated = mixed * jax.nn.silu(gate_input.astype(jnp.float32))
    squares = jnp.sum(gated * gated, axis=1)
    scaled = (gated * norm_gain[None, :]).astype(jnp.bfloat16)
    projected = jnp.dot(scaled, out_weight, preferred_element_type=jnp.float32)
    owned = lax.psum_scatter(
        projected.astype(jnp.bfloat16), "exp", scatter_dimension=0, tiled=True
    ).astype(jnp.float32)
    owned_squares = lax.psum_scatter(squares, "exp", scatter_dimension=0, tiled=True)
    mamba_out = owned * lax.rsqrt(owned_squares / INNER + EPS)[:, None]
    hidden = residual.astype(jnp.float32) + mamba_out
    tokens = hidden.shape[0]
    flight = lax.axis_size("exp")
    capacity = max(2, 2 * tokens * TOPK // NEXP)
    normed = (
        hidden * lax.rsqrt(jnp.mean(hidden * hidden, axis=1) + EPS)[:, None] * moe_gain[None, :]
    ).astype(jnp.bfloat16)
    logits = jnp.dot(normed, router_weight, preferred_element_type=jnp.float32)
    table = routes[:, :, None] == jnp.arange(NEXP, dtype=jnp.int32)[None, None, :]
    picked = jnp.sum(jnp.where(table, logits[:, None, :], 0.0), axis=2)
    raised = jnp.exp(picked)
    probs = raised / jnp.sum(raised, axis=1, keepdims=True)
    match = routes[:, :, None] == jnp.arange(flight, dtype=jnp.int32)[None, None, :]
    member = jnp.sum(match.astype(jnp.int32), axis=1)
    share = jnp.sum(jnp.where(match, probs[:, :, None], 0.0), axis=1).astype(jnp.bfloat16)
    order = priority[0]
    earlier = (order[None, :] < order[:, None]).astype(jnp.int32)
    rank = jnp.sum(earlier[:, :, None] * member[None, :, :], axis=1)
    kept = (member > 0) & (rank < capacity)
    slots = kept[:, :, None] & (
        rank[:, :, None] == jnp.arange(capacity, dtype=jnp.int32)[None, None, :]
    )
    select = jnp.transpose(slots, (1, 2, 0)).astype(jnp.bfloat16)
    outbound = jnp.einsum("fst,td->fsd", select, normed, preferred_element_type=jnp.float32).astype(
        jnp.bfloat16
    )
    arrived = lax.all_to_all(outbound, "exp", split_axis=0, concat_axis=0, tiled=True)
    rows = arrived.reshape(flight * capacity, normed.shape[1])
    slices = lax.axis_size("ctx")
    whole_in = lax.all_gather(expert_in[0], "ctx", axis=0, tiled=True)
    slice_width = rows.shape[1] // slices
    parts = jnp.einsum(
        "rkw,kwf->krf",
        rows.reshape(rows.shape[0], slices, slice_width),
        whole_in.reshape(slices, slice_width, 2 * FFE),
        preferred_element_type=jnp.float32,
    ).astype(jnp.bfloat16)
    units = jnp.sum(lax.optimization_barrier(parts).astype(jnp.float32), axis=0)
    activated = (jax.nn.silu(units[:, :FFE]) * units[:, FFE:]).astype(jnp.bfloat16)
    answer = jnp.einsum(
        "rf,df->rd",
        activated,
        lax.all_gather(expert_out[0], "ctx", axis=0, tiled=True),
        preferred_element_type=jnp.float32,
    ).astype(jnp.bfloat16)
    returned = lax.all_to_all(
        answer.reshape(flight, capacity, answer.shape[1]),
        "exp",
        split_axis=0,
        concat_axis=0,
        tiled=True,
    )
    weights = select * jnp.transpose(share)[:, None, :]
    moe_out = jnp.einsum("fst,fsd->td", weights, returned, preferred_element_type=jnp.float32)
    return (hidden, moe_out)


def solution(mesh):
    placed = (
        P("ctx", "exp"),
        P("ctx", "exp"),
        P("ctx", None),
        P("ctx", "exp"),
        P(None, "exp"),
        P(),
        P("exp"),
        P("exp"),
        P("exp"),
        P("exp", None),
        P(("ctx", "exp"), None),
        P(),
        P(),
        P(("ctx", "exp"), None),
        P(("ctx", "exp"), None),
        P("exp", "ctx", None),
        P("exp", "ctx", None),
    )
    return jax.shard_map(
        body,
        mesh=mesh,
        in_specs=placed,
        out_specs=(P(("ctx", "exp"), None), P(("ctx", "exp"), None)),
        check_vma=False,
    )
```

profile of v0, /device:TPU:32, one launch (start us, length us, event | category | flops | bytes accessed | tf_op | source)
XLA Modules:
  0.0 354.1 jit_solution(14720117451480724429)
XLA Ops:
  9.5 1.9 collective-permute-start
  12.9 1.1 reduce-window.6
  17.5 1.0 convert_element_type.80
  18.5 1.3 copy.92
  20.4 1.5 multiply_convert_fusion.9
  23.8 19.0 %all-gather.2 = f32[16,1,8]{2,1,0:T(1,128)} all-gather(f32[1,1,8]{2,1,0:T(1,128)S(1)} %get-tuple-element.98), channel_id=1, replica_groups=mesh['ctx'=16,'exp'=16] {'ctx'}, dimensions={0}, use_global_device_ids=true | all-gather | bytes 544 | tf_op jit(solution)/shard_map/all_gather | solution.py:26
  43.5 1.0 fusion.67
  44.6 24.1 %all-gather.7.cloned.1.call-done = f32[16,8,128,64]{2,3,1,0:T(8,128)} async-done(((f32[1,8,128,64]{2,3,1,0:T(8,128)}), f32[16,8,128,64]{2,3,1,0:T(8,128)}) %all-gather.7.cloned.1.call-update) | async-done | bytes 4194320 | tf_op jit(solution)/shard_map/all_gather | solution.py:26
  68.7 4.1 %while.12 = (s32[]{:T(128)}, f32[8,128,64]{2,1,0:T(8,128)S(1)}, s32[]{:T(128)}, f32[16,8]{1,0:T(8,128)}, f32[16,8,128,64]{2,3,1,0:T(8,128)}, /*index=5*/s32[]{:T(128)}, s32[]{:T(128)}, s32[]{:T(128)}) while((s32[]{:T(128)}, f32[8,128,64]{2,1,0:T(8,128)S(1)}, s32[]{:T(128)}, f32[16,8]{1,0:T(8,128)}, f32[16,8,128,64]{2,3,1,0:T(8,128)}, ...), condition=%wide.region_3.4_spmd, body=%wide.region_2.3_spmd.sunk | while | flops 131077 | bytes 1835231 | solution.py:34
  73.9 1.5 fusion.68
  75.4 2.3 fusion.17
  78.6 1.3 copy-done.10
  79.9 4.6 %convolution_convert_fusion = bf16[512,4096]{1,0:T(8,128)(2,1)} fusion(bf16[512,4096]{1,0:T(8,128)(2,1)S(1)} %copy-done.10, f32[512]{0:T(512)S(1)} %copy-done.11, f32[512,512]{0,1:T(8,128)S(1)} %bitcast.109, bf16[512,512]{0,1:T(8,128)(2,1)S(1)} %copy.102), kind=kOutput, calls=%fused_computation.6 | convolution fusion | flops 2151677952 | bytes 9963520 | tf_op jit(solution)/shard_map/dot_general | solution.py:121
  88.4 40.4 %all-reduce = f32[512]{0:T(512)S(1)} all-reduce(f32[512]{0:T(512)S(1)} %multiply_reduce_fusion), channel_id=5, replica_groups=mesh['ctx'=16,'exp'=16] {'exp'}, use_global_device_ids=true, to_apply=%region_6.7.clone | all-reduce | flops 512 | bytes 4096
  128.9 63.8 %reduce-scatter.2.cloned.1.call-done = bf16[32,4096]{1,0:T(8,128)(2,1)} async-done(((bf16[512,4096]{1,0:T(8,128)(2,1)}), bf16[32,4096]{1,0:T(8,128)(2,1)}) %reduce-scatter.2.cloned.1.call-update) | async-done | bytes 262160 | tf_op jit(solution)/shard_map/reduce_scatter | solution.py:122
  192.6 1.2 multiply_reduce_fusion.1
  194.4 19.8 %all_to_all.10 = bf16[16,8,4096]{2,1,0:T(8,128)(2,1)S(1)} all-to-all(bf16[16,8,4096]{2,1,0:T(8,128)(2,1)S(1)} %convolution_convert_fusion.2), channel_id=1, replica_groups=mesh['ctx'=16,'exp'=16] {'exp'}, dimensions={0} | all-to-all | bytes 2097152 | tf_op jit(solution)/shard_map/all_to_all | solution.py:153
  214.5 53.0 %all-gather.9.cloned.1.call-done = bf16[1,4096,1536]{2,1,0:T(8,128)(2,1)} async-done(((bf16[1,256,1536]{2,1,0:T(8,128)(2,1)}), bf16[1,4096,1536]{2,1,0:T(8,128)(2,1)}) %all-gather.9.cloned.1.call-update) | async-done | bytes 12582928 | tf_op jit(solution)/shard_map/all_gather | solution.py:156
  267.5 6.6 %convolution_convert_fusion.1 = bf16[16,128,1536]{2,1,0:T(8,128)(2,1)S(1)} fusion(bf16[16,256,1536]{2,1,0:T(8,128)(2,1)} %bitcast.107, bf16[128,16,256]{2,1,0:T(8,128)(2,1)S(1)} %bitcast.108), kind=kOutput, calls=%fused_computation.7 | convolution fusion | flops 1613758464 | bytes 19922944 | tf_op jit(solution)/shard_map/rkw,kwf->krf/dot_general | solution.py:158
  275.0 40.1 %all-gather.11.cloned.1.call-done = bf16[1,4096,768]{2,1,0:T(8,128)(2,1)} async-done(((bf16[1,256,768]{2,1,0:T(8,128)(2,1)}), bf16[1,4096,768]{2,1,0:T(8,128)(2,1)}) %all-gather.11.cloned.1.call-update) | async-done | bytes 6291472 | tf_op jit(solution)/shard_map/all_gather | solution.py:169
  315.1 5.9 %fusion.5 = bf16[16,8,4096]{2,1,0:T(8,128)(2,1)} fusion(bf16[1,4096,768]{2,1,0:T(8,128)(2,1)} %all-gather.11.cloned.1.call-done, f32[128,1536]{1,0:T(8,128)S(1)} %convert_reduce_fusion), kind=kOutput, calls=%fused_computation.10 | convolution fusion | flops 806420480 | bytes 8126464 | tf_op jit(solution)/shard_map/rf,df->rd/dot_general | solution.py:166
  321.0 6.8 %all-to-all-start.1 = ((bf16[16,8,4096]{2,1,0:T(8,128)(2,1)}), bf16[16,8,4096]{2,1,0:T(8,128)(2,1)S(1)}, u32[]{:S(2)}, u32[]{:S(2)}) async-start(bf16[16,8,4096]{2,1,0:T(8,128)(2,1)} %fusion.5), calls=%async_computation.2 | async-start | bytes 2097152 | tf_op jit(solution)/shard_map/all_to_all | solution.py:172
  328.4 17.6 %all-to-all-done.1 = bf16[16,8,4096]{2,1,0:T(8,128)(2,1)S(1)} async-done(((bf16[16,8,4096]{2,1,0:T(8,128)(2,1)}), bf16[16,8,4096]{2,1,0:T(8,128)(2,1)S(1)}, u32[]{:S(2)}, u32[]{:S(2)}) %all-to-all-start.1) | async-done | bytes 1048608 | tf_op jit(solution)/shard_map/all_to_all | solution.py:172
  346.0 1.5 convolution_bitcast_fusion
  (97 shorter events, 21.7 us)
Async XLA Ops:
  7.2 320.6 %copy-start = (bf16[4096,72]{0,1:T(8,128)(2,1)S(1)}, bf16[4096,72]{0,1:T(8,128)(2,1)}, u32[]{:S(2)}) copy-start(bf16[4096,72]{0,1:T(8,128)(2,1)} %param.31) | copy-start | bytes 1769476
  7.2 61.5 %all-gather.7.cloned.1.call-start = ((), (), s32[]{:S(2)}) async-start(), calls=%async_computation.3 | async-start | bytes 4456448 | tf_op jit(solution)/shard_map/all_gather | solution.py:26
  9.5 10.3 %collective-permute-start = (bf16[3,768]{0,1:T(8,128)(2,1)}, bf16[3,768]{0,1:T(8,128)(2,1)S(1)}, u32[]{:S(2)}, u32[]{:S(2)}) collective-permute-start(bf16[3,768]{0,1:T(8,128)(2,1)} %copy.91), channel_id=1, source_target_pairs={{0,16},{16,32},{32,48},{48,64},{64,80},{80,96},{96,112},{112,128},... | collective-permute-start | bytes 13832 | tf_op jit(solution)/shard_map/ppermute | solution.py:21
  17.5 5.2 %copy-start.8 = (f32[8]{0:T(128)}, f32[8]{0:T(128)S(1)}, u32[]{:S(2)}) copy-start(f32[8]{0:T(128)S(1)} %broadcast_multiply_fusion) | copy-start | bytes 100
  19.7 3.9 %copy-start.4 = (bf16[512,512]{1,0:T(8,128)(2,1)S(1)}, bf16[512,512]{1,0:T(8,128)(2,1)}, u32[]{:S(2)}) copy-start(bf16[512,512]{1,0:T(8,128)(2,1)} %param.20) | copy-start | bytes 1572868
  20.4 48.3 %copy-start.2 = (bf16[512,128]{1,0:T(8,128)(2,1)}, bf16[512,128]{1,0:T(8,128)(2,1)S(1)}, u32[]{:S(2)}) copy-start(bf16[512,128]{1,0:T(8,128)(2,1)S(1)} %get-tuple-element.87) | copy-start | bytes 393220
  23.5 169.1 %reduce-scatter.2.cloned.1.call-start = ((), (), s32[]{:S(2)}) async-start(), calls=%async_computation.4 | async-start | bytes 4456448 | tf_op jit(solution)/shard_map/reduce_scatter | solution.py:122
  72.8 2.5 copy-start.3
  77.7 2.2 copy-start.10
  77.7 2.2 copy-start.11
  84.5 1.4 copy-start.6
  84.5 1.4 copy-start.9
  84.5 2.2 copy-start.12
  84.5 108.1 %copy-start.5 = (bf16[32,4096]{1,0:T(8,128)(2,1)S(1)}, bf16[32,4096]{1,0:T(8,128)(2,1)}, u32[]{:S(2)}) copy-start(bf16[32,4096]{1,0:T(8,128)(2,1)} %param.29) | copy-start | bytes 786436
  84.6 109.3 %copy-start.7 = (f32[4096]{0:T(1024)S(1)}, f32[4096]{0:T(1024)}, u32[]{:S(2)}) copy-start(f32[4096]{0:T(1024)} %param.30) | copy-start | bytes 49156
  84.6 182.9 %all-gather.9.cloned.1.call-start = ((), (), s32[]{:S(2)}) async-start(), calls=%async_computation.5 | async-start | bytes 13369344 | tf_op jit(solution)/shard_map/all_gather | solution.py:156
  85.3 229.7 %all-gather.11.cloned.1.call-start = ((), (), s32[]{:S(2)}) async-start(), calls=%async_computation.6 | async-start | bytes 6684672 | tf_op jit(solution)/shard_map/all_gather | solution.py:169
  193.9 133.9 %copy-start.1 = (f32[32,4096]{1,0:T(8,128)}, f32[32,4096]{1,0:T(8,128)S(1)}, u32[]{:S(2)}) copy-start(f32[32,4096]{1,0:T(8,128)S(1)} %get-tuple-element.83) | copy-start | bytes 1572868
  321.0 25.0 %all-to-all-start.1 = ((bf16[16,8,4096]{2,1,0:T(8,128)(2,1)}), bf16[16,8,4096]{2,1,0:T(8,128)(2,1)S(1)}, u32[]{:S(2)}, u32[]{:S(2)}) async-start(bf16[16,8,4096]{2,1,0:T(8,128)(2,1)} %fusion.5), calls=%async_computation.2 | async-start | bytes 2097152 | tf_op jit(solution)/shard_map/all_to_all | solution.py:172
Sparse Core Ops, SparseCore 0:
  23.6 44.9 all-gather.6
  84.7 107.8 reduce-scatter.1
  194.5 72.9 all-gather.8
  269.2 45.8 all-gather.10
where the time goes:
time: 356 us; the launch traced here: 354 us
  waiting for transfers between devices  200 us (56%)
  blocking collectives  79.3 us (22%)
  matrix products  25.1 us (7%)
  between operations  14.8 us (4%)
  local copies, waits for them, and re-layouts  13.1 us (4%)
  other arithmetic  13.1 us (4%)
  starting transfers between devices  8.84 us (2%)
    reduce_scatter x1, waiting for transfers between devices, body(): lax.psum_scatter(projected.astype(jnp.bfloat16), 'exp', scatter_dimension...  63.8 us
    all_gather x1, waiting for transfers between devices, body(): whole_in = lax.all_gather(expert_in[0], 'ctx', axis=0, tiled=True)  53 us
    unnamed x1, blocking collectives  40.4 us
    all_gather x1, waiting for transfers between devices, body(): lax.all_gather(expert_out[0], 'ctx', axis=0, tiled=True)  40.1 us
    all_gather x1, waiting for transfers between devices, carried_in(): gathered = jax.tree.map(lambda a: lax.all_gather(a, axis), part)  24.1 us
    all_to_all x1, blocking collectives, body(): lax.all_to_all(outbound, 'exp', split_axis=0, concat_axis=0, tiled=True)  19.8 us
    all_gather x1, blocking collectives, carried_in(): gathered = jax.tree.map(lambda a: lax.all_gather(a, axis), part)  19 us
    all_to_all x1, waiting for transfers between devices, body(): lax.all_to_all(answer.reshape(flight, capacity, answer.shape[1]), 'exp',...  17.6 us
  transfers between devices with their start and end apart: 6, of which 5 were waited for; matrix products, arithmetic and copies ran while one was open for 6% of the time, Pallas kernels for 0%

commit v1 on v0

--- a/solution.py
+++ b/solution.py
@@ -163,11 +163,43 @@
     ).astype(jnp.bfloat16)
     units = jnp.sum(lax.optimization_barrier(parts).astype(jnp.float32), axis=0)
     activated = (jax.nn.silu(units[:, :FFE]) * units[:, FFE:]).astype(jnp.bfloat16)
-    answer = jnp.einsum(
-        "rf,df->rd",
-        activated,
-        lax.all_gather(expert_out[0], "ctx", axis=0, tiled=True),
-        preferred_element_type=jnp.float32,
+
+    def apply_limits(mat, across, local_block):
+        e_next, current_arr, res = (
+            jax.lax.axis_size(across),
+            jax.lax.axis_index(across),
+            mat.shape[0],
+        )
+        a_now, even = ([], [])
+        no = 0
+        found_now = value_now = mat
+        while no < e_next // 2 + 1:
+            a_now.append(local_block(found_now, (current_arr - no) % e_next * res))
+            if 0 < no < e_next - e_next // 2:
+                even.append(local_block(value_now, (current_arr + no) % e_next * res))
+            found_now = jax.lax.ppermute(
+                found_now,
+                axis_name=across,
+                perm=tuple(((i0, (i0 + 1) % e_next) for i0 in range(e_next))),
+            )
+            value_now = jax.lax.ppermute(
+                value_now,
+                axis_name=across,
+                perm=tuple(((i0, (i0 - 1) % e_next) for i0 in range(e_next))),
+            )
+            no = no + 1
+        return jnp.roll(
+            jnp.concatenate([*a_now[::-1], *even], 1),
+            (current_arr - e_next // 2) * a_now[0].shape[1],
+            1,
+        )
+
+    answer = apply_limits(
+        expert_out[0],
+        "ctx",
+        local_block=lambda part_2, offset: jnp.einsum(
+            "rf,df->rd", activated, part_2, preferred_element_type=jnp.float32
+        ),
     ).astype(jnp.bfloat16)
     returned = lax.all_to_all(
         answer.reshape(flight, capacity, answer.shape[1]),

time: 356 us -> 325 us (0.913)
  waiting for transfers between devices: 200 us -> 150 us
  starting transfers between devices: 8.84 us -> 38.9 us
  blocking collectives: 79.3 us -> 58.5 us
  matrix products: 25.1 us -> 32.1 us
    reduce_scatter x1, waiting for transfers between devices: 63.8 us -> 15 us  [body(): lax.psum_scatter(projected.astype(jnp.bfloat16), 'exp', scatter_dimension...]
    ppermute x0 -> x15, waiting for transfers between devices: none -> 42.6 us  [the longest x8 21.9 us: apply_limits(): jax.lax.ppermute(found_now, axis_name=across, perm=tuple(((i0, (i0 + 1) %...]
    all_gather x1 -> x0, waiting for transfers between devices: 40.1 us -> none  [body(): lax.all_gather(expert_out[0], 'ctx', axis=0, tiled=True)]
    ppermute x0 -> x15, starting transfers between devices: none -> 24.9 us  [the longest x7 21.1 us: apply_limits(): jax.lax.ppermute(value_now, axis_name=across, perm=tuple(((i0, (i0 - 1) %...]
    all_to_all x1 -> x0, blocking collectives: 19.8 us -> none  [body(): lax.all_to_all(outbound, 'exp', split_axis=0, concat_axis=0, tiled=True)]
    dot_general x1 -> x16, matrix products: 5.92 us -> 13.8 us  [body(): jnp.einsum('rf,df->rd', activated, part_2, preferred_element_type=jnp.flo...]
    all_to_all x0 -> x1, starting transfers between devices: none -> 4.8 us  [body(): lax.all_to_all(outbound, 'exp', split_axis=0, concat_axis=0, tiled=True)]
    all_gather x1, waiting for transfers between devices: 53 us -> 49.1 us  [body(): whole_in = lax.all_gather(expert_in[0], 'ctx', axis=0, tiled=True)]
  transfers between devices with their start and end apart: 6 -> 21, of which waited for: 5 -> 13; matrix products, arithmetic and copies ran while one was open for 6% -> 11% of each run, Pallas kernels for 0% -> 0%
where the time goes in v1:
time: 325 us; the launch traced here: 323 us
  waiting for transfers between devices  150 us (46%)
  blocking collectives  58.5 us (18%)
  starting transfers between devices  38.9 us (12%)
  matrix products  32.1 us (10%)
  between operations  15.2 us (5%)
  other arithmetic  14.1 us (4%)
  local copies, waits for them, and re-layouts  13.6 us (4%)
    all_gather x1, waiting for transfers between devices, body(): whole_in = lax.all_gather(expert_in[0], 'ctx', axis=0, tiled=True)  49.1 us
    unnamed x1, blocking collectives  40.6 us
    all_gather x1, waiting for transfers between devices, carried_in(): gathered = jax.tree.map(lambda a: lax.all_gather(a, axis), part)  25.3 us
    ppermute x8, waiting for transfers between devices, apply_limits(): jax.lax.ppermute(found_now, axis_name=across, perm=tuple(((i0, (i0 + 1) %...  21.9 us
    ppermute x7, starting transfers between devices, apply_limits(): jax.lax.ppermute(value_now, axis_name=across, perm=tuple(((i0, (i0 - 1) %...  21.1 us
    ppermute x7, waiting for transfers between devices, apply_limits(): jax.lax.ppermute(value_now, axis_name=across, perm=tuple(((i0, (i0 - 1) %...  20.7 us
    all_gather x1, blocking collectives, carried_in(): gathered = jax.tree.map(lambda a: lax.all_gather(a, axis), part)  17.9 us
    all_to_all x1, waiting for transfers between devices, body(): lax.all_to_all(answer.reshape(flight, capacity, answer.shape[1]), 'exp',...  17.6 us
  transfers between devices with their start and end apart: 21, of which 13 were waited for; matrix products, arithmetic and copies ran while one was open for 11% of the time, Pallas kernels for 0%

profile of v1, /device:TPU:32, one launch (start us, length us, event | category | flops | bytes accessed | tf_op | source)
XLA Modules:
  0.0 322.8 jit_solution(17004461405221099722)
XLA Ops:
  8.9 1.9 collective-permute-start
  20.3 2.2 multiply_convert_fusion.9
  25.3 17.9 %all-gather.1 = f32[16,1,8]{2,1,0:T(1,128)S(1)} all-gather(f32[1,1,8]{2,1,0:T(1,128)S(1)} %copy-done.28), channel_id=1, replica_groups=mesh['ctx'=16,'exp'=16] {'ctx'}, dimensions={0}, use_global_device_ids=true | all-gather | bytes 544 | tf_op jit(solution)/shard_map/all_gather | solution.py:26
  44.9 25.3 %all-gather.5.cloned.1.call-done = f32[16,8,128,64]{2,3,1,0:T(8,128)} async-done(((f32[1,8,128,64]{2,3,1,0:T(8,128)}), f32[16,8,128,64]{2,3,1,0:T(8,128)}) %all-gather.5.cloned.1.call-update) | async-done | bytes 4194320 | tf_op jit(solution)/shard_map/all_gather | solution.py:26
  70.2 2.8 while.12
  78.2 4.5 %convolution_convert_fusion = bf16[512,4096]{1,0:T(8,128)(2,1)} fusion(bf16[512,4096]{1,0:T(8,128)(2,1)S(1)} %copy-done.29, f32[512]{0:T(512)S(1)} %copy-done.30, f32[512,512]{0,1:T(8,128)S(1)} %bitcast.138, bf16[512,512]{0,1:T(8,128)(2,1)S(1)} %copy.102), kind=kOutput, calls=%fused_computation.4 | convolution fusion | flops 2151677952 | bytes 9963520 | tf_op jit(solution)/shard_map/dot_general | solution.py:121
  85.5 5.5 %collective-permute-done.1 = bf16[256,768]{1,0:T(8,128)(2,1)S(1)} collective-permute-done((bf16[256,768]{1,0:T(8,128)(2,1)S(1)}, bf16[256,768]{1,0:T(8,128)(2,1)S(1)}, u32[]{:S(2)}, u32[]{:S(2)}) %collective-permute-start.1) | collective-permute-done | bytes 393248 | tf_op jit(solution)/shard_map/ppermute | solution.py:180
  92.7 5.4 %collective-permute-done.2 = bf16[256,768]{1,0:T(8,128)(2,1)S(1)} collective-permute-done((bf16[256,768]{1,0:T(8,128)(2,1)S(1)}, bf16[256,768]{1,0:T(8,128)(2,1)S(1)}, u32[]{:S(2)}, u32[]{:S(2)}) %collective-permute-start.2) | collective-permute-done | bytes 393248 | tf_op jit(solution)/shard_map/ppermute | solution.py:180
  101.1 12.1 %collective-permute-start.11 = (bf16[256,768]{1,0:T(8,128)(2,1)S(1)}, bf16[256,768]{1,0:T(8,128)(2,1)}, u32[]{:S(2)}, u32[]{:S(2)}) collective-permute-start(bf16[256,768]{1,0:T(8,128)(2,1)S(1)} %collective-permute-done.10), channel_id=1, source_target_pairs={{0,240},{16,0},{32,16},{48,32},{64,48},{80,64},{96,80},{112,96},{1... | collective-permute-start | bytes 1179656 | tf_op jit(solution)/shard_map/ppermute | solution.py:185
  113.2 3.5 %collective-permute-done.3 = bf16[256,768]{1,0:T(8,128)(2,1)} collective-permute-done((bf16[256,768]{1,0:T(8,128)(2,1)S(1)}, bf16[256,768]{1,0:T(8,128)(2,1)}, u32[]{:S(2)}, u32[]{:S(2)}) %collective-permute-start.3) | collective-permute-done | bytes 393248 | tf_op jit(solution)/shard_map/ppermute | solution.py:180
  116.7 1.8 collective-permute-done.11
  118.5 3.4 %collective-permute-start.12 = (bf16[256,768]{1,0:T(8,128)(2,1)}, bf16[256,768]{1,0:T(8,128)(2,1)}, u32[]{:S(2)}, u32[]{:S(2)}) collective-permute-start(bf16[256,768]{1,0:T(8,128)(2,1)} %collective-permute-done.11), channel_id=1, source_target_pairs={{0,240},{16,0},{32,16},{48,32},{64,48},{80,64},{96,80},{112,96},{1... | collective-permute-start | bytes 1179656 | tf_op jit(solution)/shard_map/ppermute | solution.py:185
  121.8 4.3 %collective-permute-done.4 = bf16[256,768]{1,0:T(8,128)(2,1)} collective-permute-done((bf16[256,768]{1,0:T(8,128)(2,1)}, bf16[256,768]{1,0:T(8,128)(2,1)}, u32[]{:S(2)}, u32[]{:S(2)}) %collective-permute-start.4) | collective-permute-done | bytes 393248 | tf_op jit(solution)/shard_map/ppermute | solution.py:180
  126.5 40.6 %all-reduce = f32[512]{0:T(512)S(1)} all-reduce(f32[512]{0:T(512)S(1)} %multiply_reduce_fusion), channel_id=4, replica_groups=mesh['ctx'=16,'exp'=16] {'exp'}, use_global_device_ids=true, to_apply=%region_6.7.clone | all-reduce | flops 512 | bytes 4096
  167.2 15.0 %reduce-scatter.2.cloned.1.call-done = bf16[32,4096]{1,0:T(8,128)(2,1)} async-done(((bf16[512,4096]{1,0:T(8,128)(2,1)}), bf16[32,4096]{1,0:T(8,128)(2,1)}) %reduce-scatter.2.cloned.1.call-update) | async-done | bytes 262160 | tf_op jit(solution)/shard_map/reduce_scatter | solution.py:122
  185.0 4.8 %all-to-all-start = ((bf16[16,8,4096]{2,1,0:T(8,128)(2,1)}), bf16[16,8,4096]{2,1,0:T(8,128)(2,1)S(1)}, u32[]{:S(2)}, u32[]{:S(2)}) async-start(bf16[16,8,4096]{2,1,0:T(8,128)(2,1)} %convolution_convert_fusion.2), calls=%async_computation.1 | async-start | bytes 2097152 | tf_op jit(solution)/shard_map/all_to_all | solution.py:153
  190.3 6.9 %collective-permute-done.13 = bf16[256,768]{1,0:T(8,128)(2,1)S(1)} collective-permute-done((bf16[256,768]{1,0:T(8,128)(2,1)}, bf16[256,768]{1,0:T(8,128)(2,1)S(1)}, u32[]{:S(2)}, u32[]{:S(2)}) %collective-permute-start.13) | collective-permute-done | bytes 393248 | tf_op jit(solution)/shard_map/ppermute | solution.py:185
  197.2 2.2 collective-permute-start.14
  201.2 12.1 %collective-permute-done.14 = bf16[256,768]{1,0:T(8,128)(2,1)} collective-permute-done((bf16[256,768]{1,0:T(8,128)(2,1)S(1)}, bf16[256,768]{1,0:T(8,128)(2,1)}, u32[]{:S(2)}, u32[]{:S(2)}) %collective-permute-start.14) | collective-permute-done | bytes 393248 | tf_op jit(solution)/shard_map/ppermute | solution.py:185
  213.3 2.3 collective-permute-start.15
  217.3 49.1 %all-gather.7.cloned.1.call-done = bf16[1,4096,1536]{2,1,0:T(8,128)(2,1)} async-done(((bf16[1,256,1536]{2,1,0:T(8,128)(2,1)}), bf16[1,4096,1536]{2,1,0:T(8,128)(2,1)}) %all-gather.7.cloned.1.call-update) | async-done | bytes 12582928 | tf_op jit(solution)/shard_map/all_gather | solution.py:156
  266.5 6.6 %convolution_convert_fusion.1 = bf16[16,128,1536]{2,1,0:T(8,128)(2,1)S(1)} fusion(bf16[16,256,1536]{2,1,0:T(8,128)(2,1)} %bitcast.136, bf16[128,16,256]{2,1,0:T(8,128)(2,1)S(1)} %bitcast.137), kind=kOutput, calls=%fused_computation.5 | convolution fusion | flops 1613758464 | bytes 19922944 | tf_op jit(solution)/shard_map/rkw,kwf->krf/dot_general | solution.py:158
  289.3 7.2 %all-to-all-start.1 = ((bf16[16,8,4096]{2,1,0:T(8,128)(2,1)}), bf16[16,8,4096]{2,1,0:T(8,128)(2,1)S(1)}, u32[]{:S(2)}, u32[]{:S(2)}) async-start(bf16[16,8,4096]{2,1,0:T(8,128)(2,1)} %fusion.21), calls=%async_computation.2 | async-start | bytes 2097152 | tf_op jit(solution)/shard_map/all_to_all | solution.py:204
  297.2 17.6 %all-to-all-done.1 = bf16[16,8,4096]{2,1,0:T(8,128)(2,1)S(1)} async-done(((bf16[16,8,4096]{2,1,0:T(8,128)(2,1)}), bf16[16,8,4096]{2,1,0:T(8,128)(2,1)S(1)}, u32[]{:S(2)}, u32[]{:S(2)}) %all-to-all-start.1) | async-done | bytes 1048608 | tf_op jit(solution)/shard_map/all_to_all | solution.py:204
  (198 shorter events, 55.4 us)
Async XLA Ops:
  7.2 289.4 %copy-start = (bf16[4096,72]{0,1:T(8,128)(2,1)S(1)}, bf16[4096,72]{0,1:T(8,128)(2,1)}, u32[]{:S(2)}) copy-start(bf16[4096,72]{0,1:T(8,128)(2,1)} %param.31) | copy-start | bytes 1769476
  7.2 62.9 %all-gather.5.cloned.1.call-start = ((), (), s32[]{:S(2)}) async-start(), calls=%async_computation.3 | async-start | bytes 4456448 | tf_op jit(solution)/shard_map/all_gather | solution.py:26
  8.9 10.9 %collective-permute-start = (bf16[3,768]{0,1:T(8,128)(2,1)S(1)}, bf16[3,768]{0,1:T(8,128)(2,1)S(1)}, u32[]{:S(2)}, u32[]{:S(2)}) collective-permute-start(bf16[3,768]{0,1:T(8,128)(2,1)S(1)} %copy.91), channel_id=1, source_target_pairs={{0,16},{16,32},{32,48},{48,64},{64,80},{80,96},{96,112},{112,128},... | collective-permute-start | bytes 13832 | tf_op jit(solution)/shard_map/ppermute | solution.py:21
  25.0 157.2 %reduce-scatter.2.cloned.1.call-start = ((), (), s32[]{:S(2)}) async-start(), calls=%async_computation.4 | async-start | bytes 4456448 | tf_op jit(solution)/shard_map/reduce_scatter | solution.py:122
  82.8 100.7 %copy-start.23 = (f32[4096]{0:T(1024)S(1)}, f32[4096]{0:T(1024)}, u32[]{:S(2)}) copy-start(f32[4096]{0:T(1024)} %param.30) | copy-start | bytes 49156
  82.8 183.7 %all-gather.7.cloned.1.call-start = ((), (), s32[]{:S(2)}) async-start(), calls=%async_computation.5 | async-start | bytes 13369344 | tf_op jit(solution)/shard_map/all_gather | solution.py:156
  83.7 7.2 %collective-permute-start.1 = (bf16[256,768]{1,0:T(8,128)(2,1)S(1)}, bf16[256,768]{1,0:T(8,128)(2,1)S(1)}, u32[]{:S(2)}, u32[]{:S(2)}) collective-permute-start(bf16[256,768]{1,0:T(8,128)(2,1)S(1)} %bitcast.149), channel_id=1, source_target_pairs={{0,16},{16,32},{32,48},{48,64},{64,80},{80,96},{96,112},{112,128},... | collective-permute-start | bytes 1179656 | tf_op jit(solution)/shard_map/ppermute | solution.py:180
  85.3 6.5 %collective-permute-start.9 = (bf16[256,768]{1,0:T(8,128)(2,1)S(1)}, bf16[256,768]{1,0:T(8,128)(2,1)S(1)}, u32[]{:S(2)}, u32[]{:S(2)}) collective-permute-start(bf16[256,768]{1,0:T(8,128)(2,1)S(1)} %bitcast.150), channel_id=1, source_target_pairs={{0,240},{16,0},{32,16},{48,32},{64,48},{80,64},{96,80},{112,96},{1... | collective-permute-start | bytes 1179656 | tf_op jit(solution)/shard_map/ppermute | solution.py:185
  90.9 7.2 %collective-permute-start.2 = (bf16[256,768]{1,0:T(8,128)(2,1)S(1)}, bf16[256,768]{1,0:T(8,128)(2,1)S(1)}, u32[]{:S(2)}, u32[]{:S(2)}) collective-permute-start(bf16[256,768]{1,0:T(8,128)(2,1)S(1)} %collective-permute-done.1), channel_id=1, source_target_pairs={{0,16},{16,32},{32,48},{48,64},{64,80},{80,96},{96,112},{112,128},... | collective-permute-start | bytes 1179656 | tf_op jit(solution)/shard_map/ppermute | solution.py:180
  91.8 9.2 %collective-permute-start.10 = (bf16[256,768]{1,0:T(8,128)(2,1)S(1)}, bf16[256,768]{1,0:T(8,128)(2,1)S(1)}, u32[]{:S(2)}, u32[]{:S(2)}) collective-permute-start(bf16[256,768]{1,0:T(8,128)(2,1)S(1)} %collective-permute-done.9), channel_id=1, source_target_pairs={{0,240},{16,0},{32,16},{48,32},{64,48},{80,64},{96,80},{112,96},{1... | collective-permute-start | bytes 1179656 | tf_op jit(solution)/shard_map/ppermute | solution.py:185
  98.2 18.5 %collective-permute-start.3 = (bf16[256,768]{1,0:T(8,128)(2,1)S(1)}, bf16[256,768]{1,0:T(8,128)(2,1)}, u32[]{:S(2)}, u32[]{:S(2)}) collective-permute-start(bf16[256,768]{1,0:T(8,128)(2,1)S(1)} %collective-permute-done.2), channel_id=1, source_target_pairs={{0,16},{16,32},{32,48},{48,64},{64,80},{80,96},{96,112},{112,128},... | collective-permute-start | bytes 1179656 | tf_op jit(solution)/shard_map/ppermute | solution.py:180
  101.1 17.4 %collective-permute-start.11 = (bf16[256,768]{1,0:T(8,128)(2,1)S(1)}, bf16[256,768]{1,0:T(8,128)(2,1)}, u32[]{:S(2)}, u32[]{:S(2)}) collective-permute-start(bf16[256,768]{1,0:T(8,128)(2,1)S(1)} %collective-permute-done.10), channel_id=1, source_target_pairs={{0,240},{16,0},{32,16},{48,32},{64,48},{80,64},{96,80},{112,96},{1... | collective-permute-start | bytes 1179656 | tf_op jit(solution)/shard_map/ppermute | solution.py:185
  116.6 9.5 %collective-permute-start.4 = (bf16[256,768]{1,0:T(8,128)(2,1)}, bf16[256,768]{1,0:T(8,128)(2,1)}, u32[]{:S(2)}, u32[]{:S(2)}) collective-permute-start(bf16[256,768]{1,0:T(8,128)(2,1)} %collective-permute-done.3), channel_id=1, source_target_pairs={{0,16},{16,32},{32,48},{48,64},{64,80},{80,96},{96,112},{112,128},... | collective-permute-start | bytes 1179656 | tf_op jit(solution)/shard_map/ppermute | solution.py:180
  118.5 71.3 %collective-permute-start.12 = (bf16[256,768]{1,0:T(8,128)(2,1)}, bf16[256,768]{1,0:T(8,128)(2,1)}, u32[]{:S(2)}, u32[]{:S(2)}) collective-permute-start(bf16[256,768]{1,0:T(8,128)(2,1)} %collective-permute-done.11), channel_id=1, source_target_pairs={{0,240},{16,0},{32,16},{48,32},{64,48},{80,64},{96,80},{112,96},{1... | collective-permute-start | bytes 1179656 | tf_op jit(solution)/shard_map/ppermute | solution.py:185
  126.1 63.7 %collective-permute-start.5 = (bf16[256,768]{1,0:T(8,128)(2,1)}, bf16[256,768]{1,0:T(8,128)(2,1)}, u32[]{:S(2)}, u32[]{:S(2)}) collective-permute-start(bf16[256,768]{1,0:T(8,128)(2,1)} %collective-permute-done.4), channel_id=1, source_target_pairs={{0,16},{16,32},{32,48},{48,64},{64,80},{80,96},{96,112},{112,128},... | collective-permute-start | bytes 1179656 | tf_op jit(solution)/shard_map/ppermute | solution.py:180
  183.5 113.1 %copy-start.1 = (f32[32,4096]{1,0:T(8,128)}, f32[32,4096]{1,0:T(8,128)S(1)}, u32[]{:S(2)}) copy-start(f32[32,4096]{1,0:T(8,128)S(1)} %get-tuple-element.83) | copy-start | bytes 1572868
  185.0 32.1 %all-to-all-start = ((bf16[16,8,4096]{2,1,0:T(8,128)(2,1)}), bf16[16,8,4096]{2,1,0:T(8,128)(2,1)S(1)}, u32[]{:S(2)}, u32[]{:S(2)}) async-start(bf16[16,8,4096]{2,1,0:T(8,128)(2,1)} %convolution_convert_fusion.2), calls=%async_computation.1 | async-start | bytes 2097152 | tf_op jit(solution)/shard_map/all_to_all | solution.py:153
  189.8 7.4 %collective-permute-start.13 = (bf16[256,768]{1,0:T(8,128)(2,1)}, bf16[256,768]{1,0:T(8,128)(2,1)S(1)}, u32[]{:S(2)}, u32[]{:S(2)}) collective-permute-start(bf16[256,768]{1,0:T(8,128)(2,1)} %collective-permute-done.12), channel_id=1, source_target_pairs={{0,240},{16,0},{32,16},{48,32},{64,48},{80,64},{96,80},{112,96},{1... | collective-permute-start | bytes 1179656 | tf_op jit(solution)/shard_map/ppermute | solution.py:185
  189.9 11.3 %collective-permute-start.6 = (bf16[256,768]{1,0:T(8,128)(2,1)}, bf16[256,768]{1,0:T(8,128)(2,1)S(1)}, u32[]{:S(2)}, u32[]{:S(2)}) collective-permute-start(bf16[256,768]{1,0:T(8,128)(2,1)} %collective-permute-done.5), channel_id=1, source_target_pairs={{0,16},{16,32},{32,48},{48,64},{64,80},{80,96},{96,112},{112,128},... | collective-permute-start | bytes 1179656 | tf_op jit(solution)/shard_map/ppermute | solution.py:180
  197.2 16.0 %collective-permute-start.14 = (bf16[256,768]{1,0:T(8,128)(2,1)S(1)}, bf16[256,768]{1,0:T(8,128)(2,1)}, u32[]{:S(2)}, u32[]{:S(2)}) collective-permute-start(bf16[256,768]{1,0:T(8,128)(2,1)S(1)} %collective-permute-done.13), channel_id=1, source_target_pairs={{0,240},{16,0},{32,16},{48,32},{64,48},{80,64},{96,80},{112,96},{1... | collective-permute-start | bytes 1179656 | tf_op jit(solution)/shard_map/ppermute | solution.py:185
  201.2 15.9 %collective-permute-start.7 = (bf16[256,768]{1,0:T(8,128)(2,1)S(1)}, bf16[256,768]{1,0:T(8,128)(2,1)}, u32[]{:S(2)}, u32[]{:S(2)}) collective-permute-start(bf16[256,768]{1,0:T(8,128)(2,1)S(1)} %collective-permute-done.6), channel_id=1, source_target_pairs={{0,16},{16,32},{32,48},{48,64},{64,80},{80,96},{96,112},{112,128},... | collective-permute-start | bytes 1179656 | tf_op jit(solution)/shard_map/ppermute | solution.py:180
  213.3 73.5 %collective-permute-start.15 = (bf16[256,768]{1,0:T(8,128)(2,1)}, bf16[256,768]{1,0:T(8,128)(2,1)}, u32[]{:S(2)}, u32[]{:S(2)}) collective-permute-start(bf16[256,768]{1,0:T(8,128)(2,1)} %collective-permute-done.14), channel_id=1, source_target_pairs={{0,240},{16,0},{32,16},{48,32},{64,48},{80,64},{96,80},{112,96},{1... | collective-permute-start | bytes 1179656 | tf_op jit(solution)/shard_map/ppermute | solution.py:185
  217.0 57.1 %collective-permute-start.8 = (bf16[256,768]{1,0:T(8,128)(2,1)}, bf16[256,768]{1,0:T(8,128)(2,1)}, u32[]{:S(2)}, u32[]{:S(2)}) collective-permute-start(bf16[256,768]{1,0:T(8,128)(2,1)} %collective-permute-done.7), channel_id=1, source_target_pairs={{0,16},{16,32},{32,48},{48,64},{64,80},{80,96},{96,112},{112,128},... | collective-permute-start | bytes 1179656 | tf_op jit(solution)/shard_map/ppermute | solution.py:180
  289.3 25.4 %all-to-all-start.1 = ((bf16[16,8,4096]{2,1,0:T(8,128)(2,1)}), bf16[16,8,4096]{2,1,0:T(8,128)(2,1)S(1)}, u32[]{:S(2)}, u32[]{:S(2)}) async-start(bf16[16,8,4096]{2,1,0:T(8,128)(2,1)} %fusion.21), calls=%async_computation.2 | async-start | bytes 2097152 | tf_op jit(solution)/shard_map/all_to_all | solution.py:204
  (30 other events, 452.0 us)
Sparse Core Ops, SparseCore 0:
  25.1 44.9 all-gather.4
  82.9 99.2 reduce-scatter.1
  184.0 82.3 all-gather.6
